TPU v7x, 256 devices: a whole 4x4x8 slice. The times are simulated.
256 devices in a mesh: snap: 4 (over x_hi, core), param: 64 (over x_lo, z, y).
Axes of the slice: x: 4 (x_hi: 2, x_lo: 2; x = x_hi * 2 + x_lo), y: 4, z: 8, core: 2. Of those that a mesh axis runs over, the one named last changes fastest.
Arguments:
- snap_in: float32 [32, 64, 1344], P('snap', None, 'param'), may hold values from -6 to 6
- snap_qkv: float32 [32, 1344, 4032], P('snap', 'param'), may hold values from -16 to 16
- snap_proj: float32 [32, 1344, 1344], P('snap', 'param'), may hold values from -16 to 16
- snap_out: float32 [32, 1344, 64], P('snap', 'param'), may hold values from -48 to 48
- coeffs: float32 [32, 8], P('snap'), may hold values from -3 to 3
- latent: float32 [64, 64, 256], P('param'), may hold values from -6 to 6
- levels: int32 [64], P('param'), may hold values from 0 to 15
Outputs:
- denoised: float32 [8, 64, 64, 256], P('snap', 'param')
All inputs are finite; a program needn't handle non-finite values.
Results may differ from a plain program's by a relative error of at most 0.012.
Values may be sent and summed in bfloat16 or wider, within the bound.
No kernel may reach another device: no remote copies, remote signals or barrier semaphores. Data moves between devices by JAX's collectives and lax.ppermute only.
A program may use at most 192 MiB of HBM per device.

v0:
```python
import jax
import jax.numpy as jnp
from jax import lax
from jax.sharding import Mesh, PartitionSpec as P

HEAD_DIM = 64
PROF = 8
NLEV = 16
EPS = 0.0001
SNAP = ("xh", "core")
PARAM = ("xl", "z", "y")
ZY = ("z", "y")
X = ("xh", "xl")


def noise_scales(levels):
    step = levels.astype(jnp.float32) / (NLEV - 1)
    sigma = jnp.exp(jnp.log(0.2) + step * (jnp.log(5.0) - jnp.log(0.2)))
    square = sigma * sigma + 0.25
    return (1.0 / jnp.sqrt(square), 0.25 / square, 0.5 * sigma / jnp.sqrt(square))


def to_tokens(image):
    return image.reshape(16, 4, 16, 4, 4).transpose(0, 2, 1, 3, 4).reshape(256, 64)


def from_tokens(feature):
    count = feature.shape[0]
    parts = feature.reshape(count, 16, 16, 4, 4, 4).transpose(0, 1, 3, 2, 4, 5)
    return parts.reshape(count, 64, 256)


def a2a(x, axis):
    return lax.all_to_all(x, axis, 0, 0, tiled=True)


def natural(rows):
    rows = rows.reshape(32, 2, 24, 64)[:, :, :21]
    return rows.transpose(1, 0, 2, 3).reshape(1344, 64)


def shards(snap_in, snap_qkv, snap_proj, snap_out, coeffs, latent, levels):
    f32, bf16 = (jnp.float32, jnp.bfloat16)
    mix = coeffs.reshape(8, 2, 2, 2).transpose(2, 1, 3, 0).reshape(8, 8)
    eye = jnp.eye(24, 21, dtype=f32)
    mix = (mix[:, None, None, :] * eye[None, :, :, None]).reshape(192, 168)

    def contract(x):
        return jnp.dot(mix, x, precision=lax.Precision.HIGHEST).astype(bf16)

    w_q = contract(snap_qkv.transpose(1, 0, 2).reshape(168, 4032))
    w_p = contract(snap_proj.transpose(1, 0, 2).reshape(168, 1344))
    w_o = contract(snap_out.transpose(1, 0, 2).reshape(168, 64))
    w_i = contract(snap_in.transpose(2, 0, 1).reshape(168, 64))
    pad = jnp.zeros((192, 64), bf16)
    part = jnp.concatenate([w_q, pad, w_p, pad, w_i, w_o], axis=1)
    part = a2a(part.reshape(2, 96, 5632), "core").astype(f32)
    part = (part[0] + part[1]).astype(bf16)
    part = a2a(part.reshape(4, 24, 5632), X).astype(f32)
    part = part.reshape(2, 48, 5632)
    total = part[0] + part[1]
    q, p, wi, wo = (total[:, :4096], total[:, 4096:5440], total[:, 5504:5568], total[:, 5568:])
    wi = wi / (EPS + jnp.sqrt(jnp.sum(wi * wi, axis=1, keepdims=True)))
    ww = jnp.concatenate([wi, wo], axis=1).astype(bf16)
    squares = jnp.pad(jnp.sum(p * p, axis=0), (0, 64)).reshape(11, 128)
    squares = jnp.pad(squares, ((0, 5), (0, 0))).astype(bf16)
    q = q.astype(bf16).reshape(48, 32, 128).transpose(1, 0, 2)
    same = jnp.concatenate([ww, squares], axis=0)
    send = jnp.concatenate([q, jnp.broadcast_to(same[None], (32, 64, 128))], axis=1)
    got = a2a(send, ZY)
    q = got[:, :48].reshape(1536, 128)
    wi = got[:, 48:96, :64].reshape(1536, 64)
    wo = natural(got[:, 48:96, 64:])
    qf = q.astype(f32)
    qn = 1.0 / (EPS + jnp.sqrt(jnp.sum(qf * qf, axis=0)))
    m = lax.dot_general(wi, q, (((0,), (0,)), ((), ())), preferred_element_type=f32) * qn
    of = wo.astype(f32)
    on = 1.0 / (EPS + jnp.sqrt(jnp.sum(of * of, axis=0)))
    squares = jnp.sum(got[:, 96:107].astype(f32), axis=0).reshape(1408)[:1344]
    p = (p / (EPS + jnp.sqrt(squares))).astype(bf16)
    r = jnp.dot(p, wo, preferred_element_type=f32) * on
    n = (
        lax.dot_general(
            natural(got[:, 48:96, :64]), wo, (((0,), (0,)), ((), ())), preferred_element_type=f32
        )
        * on
    )
    r = r.reshape(2, 24, 64).transpose(1, 0, 2).reshape(24, 128)
    send = jnp.concatenate([m, r], axis=0).astype(bf16)
    got = a2a(jnp.broadcast_to(send[None], (32, 88, 128)), ZY)
    m = got[:, :64].transpose(1, 0, 2).reshape(64, 4096)[:, :4032]
    r = natural(got[:, 64:].reshape(32, 24, 2, 64).transpose(0, 2, 1, 3))
    c_in, c_skip, c_out = noise_scales(levels)
    tokens = to_tokens(c_in[:, None, None] * latent).astype(bf16)
    tokens = lax.all_gather(tokens, "xl", axis=0, tiled=True)
    qkv = jnp.dot(tokens, m, preferred_element_type=f32).reshape(2, 256, 3, 21, 64)
    scale = jnp.sqrt(jnp.mean(qkv * qkv, axis=-1, keepdims=True))
    qkv = (qkv / (EPS + scale)).astype(bf16)
    query, keys, values = (qkv[:, :, 0], qkv[:, :, 1], qkv[:, :, 2])
    scores = jnp.einsum("bqhd,bkhd->bhqk", query, keys, preferred_element_type=f32)
    expo = jnp.exp(scores * (1.0 / jnp.sqrt(float(HEAD_DIM))))
    weights = (expo / jnp.sum(expo, axis=-1, keepdims=True)).astype(bf16)
    attended = jnp.einsum("bhqk,bkhd->bqhd", weights, values, preferred_element_type=f32)
    attended = attended.astype(bf16).reshape(512, 1344)
    feature = 0.3 * jnp.dot(attended, r, preferred_element_type=f32)
    feature = feature + 0.7 * jnp.dot(tokens, n.astype(bf16), preferred_element_type=f32)
    feature = feature * (1.0 / jnp.sqrt(0.58))
    feature = a2a(feature.reshape(2, 256, 64), "xl")
    image = from_tokens(feature)
    out = c_skip[:, None, None] * latent + c_out[:, None, None] * image
    return out[:, None]


def solution(mesh):
    fine = Mesh(mesh.devices.reshape(2, 2, 2, 8, 4), ("xh", "core", "xl", "z", "y"))
    in_specs = (
        P(SNAP, None, PARAM),
        P(SNAP, PARAM, None),
        P(SNAP, PARAM, None),
        P(SNAP, PARAM, None),
        P(SNAP, None),
        P(PARAM, None, None),
        P(PARAM),
    )
    out_specs = P(SNAP, PARAM, None, None)
    return jax.shard_map(shards, mesh=fine, in_specs=in_specs, out_specs=out_specs, check_vma=False)
```

profile of v0, /device:TPU:8, one launch (start us, length us, event | category | flops | bytes accessed | tf_op | source)
XLA Modules:
  0.0 165.2 jit_solution(15831513101341045576)
XLA Ops:
  0.0 0.9 copy.75
  1.0 1.0 broadcast_multiply_fusion
  2.0 1.3 mul.172
  3.3 1.2 convolution_convert_fusion.2
  4.7 1.3 convolution_convert_fusion.3
  5.9 0.7 copy.78
  6.7 2.3 %convolution_convert_fusion.1 = bf16[192,1344]{1,0:T(8,128)(2,1)S(1)} fusion(f32[192,168]{0,1:T(8,128)S(1)} %mul.172, f32[8,21,1344]{2,0,1:T(8,128)} %param.9), kind=kOutput, calls=%fused_computation.9 | convolution fusion | flops 520482816 | bytes 1548288 | tf_op jit(solution)/shard_map/dot_general | solution.py:49
  9.0 3.9 %convolution_convert_fusion = bf16[192,4032]{1,0:T(8,128)(2,1)} fusion(f32[192,168]{0,1:T(8,128)S(1)} %mul.172, f32[8,21,4032]{2,0,1:T(8,128)S(1)} %copy-done), kind=kOutput, calls=%fused_computation.7 | convolution fusion | flops 1561448448 | bytes 4386816 | tf_op jit(solution)/shard_map/dot_general | solution.py:49
  12.9 4.4 %concatenate.23 = bf16[192,5632]{1,0:T(8,128)(2,1)} concatenate(bf16[192,4032]{1,0:T(8,128)(2,1)} %convolution_convert_fusion, bf16[192,64]{1,0:T(8,128)(2,1)S(1)} %broadcast_in_dim.6, bf16[192,1344]{1,0:T(8,128)(2,1)S(1)} %convolution_convert_fusion.1, bf16[192,64]{1,0:T(8,128)(2,1)S(1)} %broadcast_in_dim.6, bf16[192,64]{1,0:T(8,128)(2,1)} %copy.78, bf16[192,64]{1,0:T(8,128)(2,1)S(1)} %copy.79), dimensions={1} | concatenate | bytes 4325376 | tf_op jit(solution)/shard_map/concatenate | solution.py:56
  17.3 6.7 %all_to_all.25 = bf16[2,96,5632]{2,1,0:T(8,128)(2,1)S(1)} all-to-all(bf16[2,96,5632]{2,1,0:T(8,128)(2,1)} %bitcast.137), channel_id=1, replica_groups=mesh['xh'=2,'core'=2,'xl'=2,'z'=8,'y'=4] {'core'}, dimensions={0} | all-to-all | bytes 4325376 | tf_op jit(solution)/shard_map/all_to_all | solution.py:34
  24.0 0.5 convert_element_type.98
  24.5 0.2 fusion.4
  24.7 19.8 %all_to_all.26 = bf16[4,24,5632]{2,1,0:T(8,128)(2,1)S(1)} all-to-all(bf16[4,24,5632]{2,1,0:T(8,128)(2,1)S(1)} %bitcast.144), channel_id=1, replica_groups=mesh['xh'=2,'core'=2,'xl'=2,'z'=8,'y'=4] {'xh','xl'}, dimensions={0} | all-to-all | bytes 2162688 | tf_op jit(solution)/shard_map/all_to_all | solution.py:34
  44.5 0.2 convert_element_type.101
  45.6 35.9 %all_to_all.27 = bf16[32,112,128]{2,1,0:T(8,128)(2,1)S(1)} all-to-all(bf16[32,112,128]{2,1,0:T(8,128)(2,1)S(1)} %pad_maximum_fusion), channel_id=1, replica_groups=mesh['xh'=2,'core'=2,'xl'=2,'z'=8,'y'=4] {'z','y'}, dimensions={0} | all-to-all | bytes 1835008 | tf_op jit(solution)/shard_map/all_to_all | solution.py:34
  81.5 0.2 fusion.29
  81.7 0.2 multiply_reduce_fusion.1
  81.9 0.2 multiply_reduce_fusion.2
  82.3 0.1 reshape.192
  82.4 1.1 fusion.14
  83.7 0.3 fusion.12
  83.9 0.9 broadcast_in_dim.8
  84.9 5.6 %all-to-all-start.3 = ((bf16[32,88,128]{2,1,0:T(8,128)(2,1)}), bf16[32,88,128]{2,1,0:T(8,128)(2,1)S(1)}, u32[]{:S(2)}, u32[]{:S(2)}) async-start(bf16[32,88,128]{2,1,0:T(8,128)(2,1)} %broadcast_in_dim.8), calls=%async_computation.3 | async-start | bytes 1441792 | tf_op jit(solution)/shard_map/all_to_all | solution.py:34
  91.4 1.2 convert_element_type.90
  92.6 2.0 %copy.74 = bf16[16,16,4,4,4]{1,0,4,3,2:T(8,128)(2,1)S(1)} copy(bf16[16,16,4,4,4]{2,0,4,3,1:T(8,128)(2,1)S(1)} %bitcast.146) | data formatting | bytes 65536 | tf_op jit(solution)/shard_map/convert_element_type | solution.py:94
  94.6 0.2 convert_element_type.92
  94.9 4.6 %all_gather.3 = bf16[512,64]{0,1:T(8,128)(2,1)S(1)} all-gather(bf16[256,64]{0,1:T(8,128)(2,1)S(1)} %convert_element_type.92), channel_id=1, replica_groups=mesh['xh'=2,'core'=2,'xl'=2,'z'=8,'y'=4] {'xl'}, dimensions={0}, use_global_device_ids=true | all-gather | bytes 98304 | tf_op jit(solution)/shard_map/all_gather | solution.py:95
  99.4 0.5 convolution_multiply_fusion.1
  99.9 10.4 %all-to-all-done.3 = bf16[32,88,128]{2,1,0:T(8,128)(2,1)S(1)} async-done(((bf16[32,88,128]{2,1,0:T(8,128)(2,1)}), bf16[32,88,128]{2,1,0:T(8,128)(2,1)S(1)}, u32[]{:S(2)}, u32[]{:S(2)}) %all-to-all-start.3) | async-done | bytes 720928 | tf_op jit(solution)/shard_map/all_to_all | solution.py:34
  110.3 0.2 reshape.197
  110.5 0.2 slice_bitcast_fusion.8
  111.0 4.4 %fusion.16 = f32[512,4032]{0,1:T(8,128)} fusion(bf16[512,64]{0,1:T(8,128)(2,1)S(1)} %all_gather.3, bf16[64,4096]{1,0:T(8,128)(2,1)S(1)} %copy_bitcast_fusion), kind=kOutput, calls=%fused_computation.38 | convolution fusion | flops 264241152 | bytes 8847360 | tf_op jit(solution)/shard_map/dot_general | solution.py:96
  115.4 10.4 %reshape.195 = f32[2,256,3,21,64]{1,0,4,3,2:T(2,128)} reshape(f32[512,4032]{0,1:T(8,128)} %fusion.16) | data formatting | bytes 16515072 | tf_op jit(solution)/shard_map/reshape | solution.py:96
  125.8 7.6 %multiply_reduce_fusion = f32[2,256,3,21]{1,0,3,2:T(2,128)S(1)} fusion(f32[2,256,3,21,64]{1,0,4,3,2:T(2,128)} %reshape.195), kind=kLoop, calls=%fused_computation.5 | loop fusion | flops 4096512 | bytes 8386560 | tf_op jit(solution)/shard_map/reduce_sum | solution.py:97
  133.4 0.2 sqrt_add_fusion
  133.6 4.6 %fusion.1 = bf16[2,256,3,21,64]{1,4,3,0,2:T(8,128)(2,1)S(1)} fusion(f32[2,256,3,21,64]{1,0,4,3,2:T(2,128)} %reshape.195, f32[2,256,3,21]{1,3,0,2:T(8,128)S(1)} %copy.84), kind=kLoop, calls=%fused_computation.4 | loop fusion | flops 4128768 | bytes 12515328 | tf_op jit(solution)/shard_map/convert_element_type | solution.py:98
  138.2 2.3 %fusion = (f32[2,21,256]{2,1,0:T(8,128)S(1)}, f32[2,21,256,256]{2,3,1,0:T(8,128)S(1)}) fusion(bf16[2,256,3,21,64]{1,4,3,0,2:T(8,128)(2,1)S(1)} %fusion.1), kind=kOutput, calls=%fused_computation.2 | convolution fusion | flops 357815808 | bytes 13805568 | tf_op jit(solution)/shard_map/bqhd,bkhd->bhqk/dot_general | solution.py:100
  140.5 2.2 %fusion.6 = bf16[2,256,21,64]{1,3,2,0:T(8,128)(2,1)S(1)} fusion(f32[2,21,256,256]{2,3,1,0:T(8,128)S(1)} %get-tuple-element.10, f32[2,21,256]{2,1,0:T(8,128)S(1)} %get-tuple-element.9, bf16[2,256,3,21,64]{1,4,3,0,2:T(8,128)(2,1)S(1)} %fusion.1), kind=kOutput, calls=%fused_computation.13 | convolution fusion | flops 361267200 | bytes 13811712 | tf_op jit(solution)/shard_map/bhqk,bkhd->bqhd/dot_general | solution.py:103
  142.7 1.4 copy.87
  144.1 0.3 copy.100
  144.4 0.4 fusion.9
  144.8 0.7 copy.116
  145.5 3.4 %all-to-all-start.4 = ((f32[2,256,64]{1,2,0:T(8,128)}), f32[2,256,64]{1,2,0:T(8,128)S(1)}, u32[]{:S(2)}, u32[]{:S(2)}) async-start(f32[2,256,64]{1,2,0:T(8,128)} %bitcast.135), calls=%async_computation.4 | async-start | bytes 262144 | tf_op jit(solution)/shard_map/all_to_all | solution.py:34
  149.0 4.3 %all-to-all-done.4 = f32[2,256,64]{1,2,0:T(8,128)S(1)} async-done(((f32[2,256,64]{1,2,0:T(8,128)}), f32[2,256,64]{1,2,0:T(8,128)S(1)}, u32[]{:S(2)}, u32[]{:S(2)}) %all-to-all-start.4) | async-done | bytes 131104 | tf_op jit(solution)/shard_map/all_to_all | solution.py:34
  153.4 1.3 mul.193
  154.7 6.0 %copy.91 = f32[2,16,4,16,4,4]{2,1,5,4,3,0:T(8,128)} copy(f32[2,16,4,16,4,4]{3,1,5,4,2,0:T(8,128)} %bitcast.145) | data formatting | bytes 262144 | tf_op jit(solution)/shard_map/mul | solution.py:110
  160.7 3.6 %mul.195 = f32[2,1,64,256]{2,3,0,1:T(8,128)S(1)} reshape(f32[2,16,4,16,4,4]{2,1,5,4,3,0:T(8,128)} %copy.91) | data formatting | bytes 262144 | tf_op jit(solution)/shard_map/mul | solution.py:110
  164.4 0.8 copy.92
  (43 shorter events, 1.7 us)
Async XLA Ops:
  0.0 9.0 %copy-start = (f32[8,21,4032]{2,0,1:T(8,128)S(1)}, f32[8,21,4032]{2,0,1:T(8,128)}, u32[]{:S(2)}) copy-start(f32[8,21,4032]{2,0,1:T(8,128)} %param.8) | copy-start | bytes 8128516
  44.8 36.7 %copy-start.2 = (f32[2,24,5632]{2,1,0:T(8,128)}, f32[2,24,5632]{2,1,0:T(8,128)S(1)}, u32[]{:S(2)}) copy-start(f32[2,24,5632]{2,1,0:T(8,128)S(1)} %slice_add_fusion.1) | copy-start | bytes 3244036
  82.2 9.1 %copy-start.3 = (f32[1,64,256]{2,1,0:T(8,128)S(1)}, f32[1,64,256]{2,1,0:T(8,128)}, u32[]{:S(2)}) copy-start(f32[1,64,256]{2,1,0:T(8,128)} %param.12) | copy-start | bytes 196612
  84.9 25.4 %all-to-all-start.3 = ((bf16[32,88,128]{2,1,0:T(8,128)(2,1)}), bf16[32,88,128]{2,1,0:T(8,128)(2,1)S(1)}, u32[]{:S(2)}, u32[]{:S(2)}) async-start(bf16[32,88,128]{2,1,0:T(8,128)(2,1)} %broadcast_in_dim.8), calls=%async_computation.3 | async-start | bytes 1441792 | tf_op jit(solution)/shard_map/all_to_all | solution.py:34
  145.5 7.8 %all-to-all-start.4 = ((f32[2,256,64]{1,2,0:T(8,128)}), f32[2,256,64]{1,2,0:T(8,128)S(1)}, u32[]{:S(2)}, u32[]{:S(2)}) async-start(f32[2,256,64]{1,2,0:T(8,128)} %bitcast.135), calls=%async_computation.4 | async-start | bytes 262144 | tf_op jit(solution)/shard_map/all_to_all | solution.py:34
  154.7 10.5 %copy-start.1 = (f32[8,21,4032]{2,0,1:T(8,128)S(1)}, f32[8,21,4032]{2,0,1:T(8,128)}, u32[]{:S(2)}) copy-start(f32[8,21,4032]{2,0,1:T(8,128)} %param.8) | copy-start | bytes 8128516
where the time goes:
time: 166 us; the launch traced here: 165 us
  blocking collectives  67 us (40%)
  local copies, waits for them, and re-layouts  38 us (23%)
  matrix products  19.9 us (12%)
  other arithmetic  15.3 us (9%)
  waiting for transfers between devices  14.7 us (9%)
  starting transfers between devices  8.94 us (5%)
    all_to_all x3, blocking collectives, a2a(): return lax.all_to_all(x, axis, 0, 0, tiled=True)  62.4 us
    all_to_all x2, waiting for transfers between devices, a2a(): return lax.all_to_all(x, axis, 0, 0, tiled=True)  14.7 us
    mul x3, local copies, waits for them, and re-layouts, shards(): out = c_skip[:, None, None] * latent + c_out[:, None, None] * image  11 us
    reshape x1, local copies, waits for them, and re-layouts, shards(): jnp.dot(tokens, m, preferred_element_type=f32).reshape(2, 256, 3, 21, 64)  10.4 us
    all_to_all x2, starting transfers between devices, a2a(): return lax.all_to_all(x, axis, 0, 0, tiled=True)  8.94 us
    dot_general x4, matrix products, contract(): return jnp.dot(mix, x, precision=lax.Precision.HIGHEST).astype(bf16)  8.75 us
    reduce_sum x1, other arithmetic, shards(): scale = jnp.sqrt(jnp.mean(qkv * qkv, axis=-1, keepdims=True))  7.56 us
    convert_element_type x1, other arithmetic, shards(): qkv = (qkv / (EPS + scale)).astype(bf16)  4.64 us
  transfers between devices with their start and end apart: 2, of which 2 were waited for; matrix products, arithmetic and copies ran while one was open for 2% of the time, Pallas kernels for 0%

commit v1 on v0

--- a/solution.py
+++ b/solution.py
@@ -92,7 +92,9 @@
     r = natural(got[:, 64:].reshape(32, 24, 2, 64).transpose(0, 2, 1, 3))
     c_in, c_skip, c_out = noise_scales(levels)
     tokens = to_tokens(c_in[:, None, None] * latent).astype(bf16)
-    tokens = lax.all_gather(tokens, "xl", axis=0, tiled=True)
+    tokens = jnp.concatenate(
+        lax.all_to_all(jnp.stack([tokens] * lax.axis_size("xl")), "xl", 0, 0), axis=0
+    )
     qkv = jnp.dot(tokens, m, preferred_element_type=f32).reshape(2, 256, 3, 21, 64)
     scale = jnp.sqrt(jnp.mean(qkv * qkv, axis=-1, keepdims=True))
     qkv = (qkv / (EPS + scale)).astype(bf16)

time: 166 us -> 148 us (0.89)
  blocking collectives: 67 us -> 26.5 us
  waiting for transfers between devices: 14.7 us -> 43.5 us
  starting transfers between devices: 8.94 us -> 23.9 us
  local copies, waits for them, and re-layouts: 38 us -> 28.7 us
  other arithmetic: 15.3 us -> 6.14 us
  matrix products: 19.9 us -> 16.8 us
    all_to_all x3 -> x2, blocking collectives: 62.4 us -> 26.5 us  [a2a(): return lax.all_to_all(x, axis, 0, 0, tiled=True)]
    all_to_all x2 -> x3, waiting for transfers between devices: 14.7 us -> 41.9 us  [a2a(): return lax.all_to_all(x, axis, 0, 0, tiled=True)]
    all_to_all x2 -> x3, starting transfers between devices: 8.94 us -> 20.6 us  [a2a(): return lax.all_to_all(x, axis, 0, 0, tiled=True)]
    reshape x1, local copies, waits for them, and re-layouts: 10.4 us -> 0.01 us  [shards(): jnp.concatenate(lax.all_to_all(jnp.stack([tokens] * lax.axis_size('xl')),...]
    reduce_sum x1 -> x0, other arithmetic: 7.56 us -> none  [shards(): scale = jnp.sqrt(jnp.mean(qkv * qkv, axis=-1, keepdims=True))]
    all_gather x1 -> x0, blocking collectives: 4.58 us -> none  [shards(): tokens = lax.all_gather(tokens, 'xl', axis=0, tiled=True)]
    all_to_all x0 -> x1, starting transfers between devices: none -> 3.3 us  [shards(): lax.all_to_all(jnp.stack([tokens] * lax.axis_size('xl')), 'xl', 0, 0)]
    dot_general x1, matrix products: 4.45 us -> 1.22 us  [shards(): jnp.dot(tokens, m, preferred_element_type=f32).reshape(2, 256, 3, 21, 64)]
  transfers between devices with their start and end apart: 2 -> 4, of which waited for: 2 -> 4; matrix products, arithmetic and copies ran while one was open for 2% -> 5% of each run, Pallas kernels for 0% -> 0%
where the time goes in v1:
time: 148 us; the launch traced here: 147 us
  waiting for transfers between devices  43.5 us (29%)
  local copies, waits for them, and re-layouts  28.7 us (19%)
  blocking collectives  26.5 us (18%)
  starting transfers between devices  23.9 us (16%)
  matrix products  16.8 us (11%)
  other arithmetic  6.14 us (4%)
    all_to_all x3, waiting for transfers between devices, a2a(): return lax.all_to_all(x, axis, 0, 0, tiled=True)  41.9 us
    all_to_all x2, blocking collectives, a2a(): return lax.all_to_all(x, axis, 0, 0, tiled=True)  26.5 us
    all_to_all x3, starting transfers between devices, a2a(): return lax.all_to_all(x, axis, 0, 0, tiled=True)  20.6 us
    mul x3, local copies, waits for them, and re-layouts, shards(): out = c_skip[:, None, None] * latent + c_out[:, None, None] * image  11 us
    dot_general x4, matrix products, contract(): return jnp.dot(mix, x, precision=lax.Precision.HIGHEST).astype(bf16)  8.75 us
    concatenate x1, local copies, waits for them, and re-layouts, shards(): part = jnp.concatenate([w_q, pad, w_p, pad, w_i, w_o], axis=1)  4.37 us
    convert_element_type x4, local copies, waits for them, and re-layouts, shards(): tokens = to_tokens(c_in[:, None, None] * latent).astype(bf16)  3.52 us
    all_to_all x1, starting transfers between devices, shards(): lax.all_to_all(jnp.stack([tokens] * lax.axis_size('xl')), 'xl', 0, 0)  3.3 us
  transfers between devices with their start and end apart: 4, of which 4 were waited for; matrix products, arithmetic and copies ran while one was open for 5% of the time, Pallas kernels for 0%

profile of v1, /device:TPU:8, one launch (start us, length us, event | category | flops | bytes accessed | tf_op | source)
XLA Modules:
  0.0 146.9 jit_solution(12033849478823803346)
XLA Ops:
  0.0 0.9 copy.76
  1.0 1.0 broadcast_multiply_fusion
  2.0 1.3 mul.172
  3.3 1.2 convolution_convert_fusion.2
  4.7 1.3 convolution_convert_fusion.3
  5.9 0.7 copy.79
  6.7 2.3 %convolution_convert_fusion.1 = bf16[192,1344]{1,0:T(8,128)(2,1)S(1)} fusion(f32[192,168]{0,1:T(8,128)S(1)} %mul.172, f32[8,21,1344]{2,0,1:T(8,128)} %param.9), kind=kOutput, calls=%fused_computation.8 | convolution fusion | flops 520482816 | bytes 1548288 | tf_op jit(solution)/shard_map/dot_general | solution.py:49
  9.0 3.9 %convolution_convert_fusion = bf16[192,4032]{1,0:T(8,128)(2,1)} fusion(f32[192,168]{0,1:T(8,128)S(1)} %mul.172, f32[8,21,4032]{2,0,1:T(8,128)S(1)} %copy-done), kind=kOutput, calls=%fused_computation.6 | convolution fusion | flops 1561448448 | bytes 4386816 | tf_op jit(solution)/shard_map/dot_general | solution.py:49
  12.9 4.4 %concatenate.23 = bf16[192,5632]{1,0:T(8,128)(2,1)} concatenate(bf16[192,4032]{1,0:T(8,128)(2,1)} %convolution_convert_fusion, bf16[192,64]{1,0:T(8,128)(2,1)S(1)} %broadcast_in_dim.6, bf16[192,1344]{1,0:T(8,128)(2,1)S(1)} %convolution_convert_fusion.1, bf16[192,64]{1,0:T(8,128)(2,1)S(1)} %broadcast_in_dim.6, bf16[192,64]{1,0:T(8,128)(2,1)} %copy.79, bf16[192,64]{1,0:T(8,128)(2,1)S(1)} %copy.80), dimensions={1} | concatenate | bytes 4325376 | tf_op jit(solution)/shard_map/concatenate | solution.py:56
  17.3 6.7 %all_to_all.30 = bf16[2,96,5632]{2,1,0:T(8,128)(2,1)S(1)} all-to-all(bf16[2,96,5632]{2,1,0:T(8,128)(2,1)} %bitcast.149), channel_id=1, replica_groups=mesh['xh'=2,'core'=2,'xl'=2,'z'=8,'y'=4] {'core'}, dimensions={0} | all-to-all | bytes 4325376 | tf_op jit(solution)/shard_map/all_to_all | solution.py:34
  24.0 0.5 convert_element_type.105
  24.5 0.2 fusion.3
  24.7 19.8 %all_to_all.31 = bf16[4,24,5632]{2,1,0:T(8,128)(2,1)S(1)} all-to-all(bf16[4,24,5632]{2,1,0:T(8,128)(2,1)S(1)} %bitcast.156), channel_id=1, replica_groups=mesh['xh'=2,'core'=2,'xl'=2,'z'=8,'y'=4] {'xh','xl'}, dimensions={0} | all-to-all | bytes 2162688 | tf_op jit(solution)/shard_map/all_to_all | solution.py:34
  44.5 0.2 convert_element_type.108
  45.2 0.6 copy-done.2
  46.1 1.0 pad_maximum_fusion
  47.1 11.7 %all-to-all-start.3 = ((bf16[32,112,128]{2,1,0:T(8,128)(2,1)}), bf16[32,112,128]{2,1,0:T(8,128)(2,1)S(1)}, u32[]{:S(2)}, u32[]{:S(2)}) async-start(bf16[32,112,128]{2,1,0:T(8,128)(2,1)} %pad_maximum_fusion), calls=%async_computation.3 | async-start | bytes 1835008 | tf_op jit(solution)/shard_map/all_to_all | solution.py:34
  59.8 1.2 convert_element_type.97
  61.0 2.0 %copy.75 = bf16[16,16,4,4,4]{1,0,4,3,2:T(8,128)(2,1)S(1)} copy(bf16[16,16,4,4,4]{2,0,4,3,1:T(8,128)(2,1)S(1)} %bitcast.158) | data formatting | bytes 65536 | tf_op jit(solution)/shard_map/convert_element_type | solution.py:94
  63.0 0.2 convert_element_type.99
  63.2 0.6 pad_maximum_fusion.1
  63.9 19.4 %all-to-all-done.3 = bf16[32,112,128]{2,1,0:T(8,128)(2,1)S(1)} async-done(((bf16[32,112,128]{2,1,0:T(8,128)(2,1)}), bf16[32,112,128]{2,1,0:T(8,128)(2,1)S(1)}, u32[]{:S(2)}, u32[]{:S(2)}) %all-to-all-start.3) | async-done | bytes 917536 | tf_op jit(solution)/shard_map/all_to_all | solution.py:34
  83.3 3.3 %all-to-all-start = ((bf16[2,256,64]{1,2,0:T(8,128)(2,1)}), bf16[2,256,64]{1,2,0:T(8,128)(2,1)S(1)}, u32[]{:S(2)}, u32[]{:S(2)}) async-start(bf16[2,256,64]{1,2,0:T(8,128)(2,1)} %pad_maximum_fusion.1), calls=%async_computation | async-start | bytes 131072 | tf_op jit(solution)/shard_map/all_to_all | solution.py:96
  86.7 0.2 multiply_reduce_fusion.1
  87.0 0.2 multiply_reduce_fusion.2
  87.5 1.2 fusion.13
  88.7 0.3 fusion.11
  89.0 1.7 %all-to-all-done = bf16[2,256,64]{1,2,0:T(8,128)(2,1)S(1)} async-done(((bf16[2,256,64]{1,2,0:T(8,128)(2,1)}), bf16[2,256,64]{1,2,0:T(8,128)(2,1)S(1)}, u32[]{:S(2)}, u32[]{:S(2)}) %all-to-all-start) | async-done | bytes 65568 | tf_op jit(solution)/shard_map/all_to_all | solution.py:96
  90.7 0.9 broadcast_in_dim.8
  91.6 5.6 %all-to-all-start.4 = ((bf16[32,88,128]{2,1,0:T(8,128)(2,1)}), bf16[32,88,128]{2,1,0:T(8,128)(2,1)S(1)}, u32[]{:S(2)}, u32[]{:S(2)}) async-start(bf16[32,88,128]{2,1,0:T(8,128)(2,1)} %broadcast_in_dim.8), calls=%async_computation.4 | async-start | bytes 1441792 | tf_op jit(solution)/shard_map/all_to_all | solution.py:34
  97.2 0.5 convolution_multiply_fusion.1
  97.7 18.2 %all-to-all-done.4 = bf16[32,88,128]{2,1,0:T(8,128)(2,1)S(1)} async-done(((bf16[32,88,128]{2,1,0:T(8,128)(2,1)}), bf16[32,88,128]{2,1,0:T(8,128)(2,1)S(1)}, u32[]{:S(2)}, u32[]{:S(2)}) %all-to-all-start.4) | async-done | bytes 720928 | tf_op jit(solution)/shard_map/all_to_all | solution.py:34
  116.1 0.2 slice_bitcast_fusion.9
  116.6 0.5 copy.85
  117.1 1.2 multiply_reduce_fusion
  118.4 1.5 %divide_convert_fusion.1 = bf16[2,256,3,21,64]{1,4,3,2,0:T(8,128)(2,1)S(1)} fusion(f32[2,256,3,21,64]{1,4,3,2,0:T(8,128)S(1)} %get-tuple-element.10, f32[2,256,3,21]{1,3,2,0:T(8,128)S(1)} %sqrt_add_fusion), kind=kLoop, calls=%fused_computation.3 | loop fusion | flops 4128768 | bytes 12515328 | tf_op jit(solution)/shard_map/convert_element_type | solution.py:100
  119.9 2.3 %fusion = (f32[2,21,256]{2,1,0:T(8,128)S(1)}, f32[2,21,256,256]{2,3,1,0:T(8,128)S(1)}) fusion(bf16[2,256,3,21,64]{1,4,3,2,0:T(8,128)(2,1)S(1)} %divide_convert_fusion.1), kind=kOutput, calls=%fused_computation.2 | convolution fusion | flops 357815808 | bytes 13805568 | tf_op jit(solution)/shard_map/bqhd,bkhd->bhqk/dot_general | solution.py:102
  122.2 2.2 %fusion.5 = bf16[2,256,21,64]{1,3,2,0:T(8,128)(2,1)S(1)} fusion(f32[2,21,256,256]{2,3,1,0:T(8,128)S(1)} %get-tuple-element.12, f32[2,21,256]{2,1,0:T(8,128)S(1)} %get-tuple-element.11, bf16[2,256,3,21,64]{1,4,3,2,0:T(8,128)(2,1)S(1)} %divide_convert_fusion.1), kind=kOutput, calls=%fused_computation.12 | convolution fusion | flops 361267200 | bytes 13811712 | tf_op jit(solution)/shard_map/bhqk,bkhd->bqhd/dot_general | solution.py:105
  124.4 1.4 copy.87
  125.8 0.3 copy.103
  126.1 0.4 fusion.8
  126.6 0.7 copy.116
  127.2 3.4 %all-to-all-start.5 = ((f32[2,256,64]{1,2,0:T(8,128)}), f32[2,256,64]{1,2,0:T(8,128)S(1)}, u32[]{:S(2)}, u32[]{:S(2)}) async-start(f32[2,256,64]{1,2,0:T(8,128)} %bitcast.147), calls=%async_computation.5 | async-start | bytes 262144 | tf_op jit(solution)/shard_map/all_to_all | solution.py:34
  130.7 4.3 %all-to-all-done.5 = f32[2,256,64]{1,2,0:T(8,128)S(1)} async-done(((f32[2,256,64]{1,2,0:T(8,128)}), f32[2,256,64]{1,2,0:T(8,128)S(1)}, u32[]{:S(2)}, u32[]{:S(2)}) %all-to-all-start.5) | async-done | bytes 131104 | tf_op jit(solution)/shard_map/all_to_all | solution.py:34
  135.1 1.3 mul.193
  136.4 6.0 %copy.92 = f32[2,16,4,16,4,4]{2,1,5,4,3,0:T(8,128)} copy(f32[2,16,4,16,4,4]{3,1,5,4,2,0:T(8,128)} %bitcast.157) | data formatting | bytes 262144 | tf_op jit(solution)/shard_map/mul | solution.py:112
  142.4 3.6 %mul.195 = f32[2,1,64,256]{2,3,0,1:T(8,128)S(1)} reshape(f32[2,16,4,16,4,4]{2,1,5,4,3,0:T(8,128)} %copy.92) | data formatting | bytes 262144 | tf_op jit(solution)/shard_map/mul | solution.py:112
  146.1 0.8 copy.93
  (46 shorter events, 2.2 us)
Async XLA Ops:
  0.0 9.0 %copy-start = (f32[8,21,4032]{2,0,1:T(8,128)S(1)}, f32[8,21,4032]{2,0,1:T(8,128)}, u32[]{:S(2)}) copy-start(f32[8,21,4032]{2,0,1:T(8,128)} %param.8) | copy-start | bytes 8128516
  44.8 1.0 copy-start.2
  45.2 14.4 %copy-start.3 = (f32[1,64,256]{2,1,0:T(8,128)S(1)}, f32[1,64,256]{2,1,0:T(8,128)}, u32[]{:S(2)}) copy-start(f32[1,64,256]{2,1,0:T(8,128)} %param.12) | copy-start | bytes 196612
  47.1 36.1 %all-to-all-start.3 = ((bf16[32,112,128]{2,1,0:T(8,128)(2,1)}), bf16[32,112,128]{2,1,0:T(8,128)(2,1)S(1)}, u32[]{:S(2)}, u32[]{:S(2)}) async-start(bf16[32,112,128]{2,1,0:T(8,128)(2,1)} %pad_maximum_fusion), calls=%async_computation.3 | async-start | bytes 1835008 | tf_op jit(solution)/shard_map/all_to_all | solution.py:34
  83.3 7.4 %all-to-all-start = ((bf16[2,256,64]{1,2,0:T(8,128)(2,1)}), bf16[2,256,64]{1,2,0:T(8,128)(2,1)S(1)}, u32[]{:S(2)}, u32[]{:S(2)}) async-start(bf16[2,256,64]{1,2,0:T(8,128)(2,1)} %pad_maximum_fusion.1), calls=%async_computation | async-start | bytes 131072 | tf_op jit(solution)/shard_map/all_to_all | solution.py:96
  91.6 24.2 %all-to-all-start.4 = ((bf16[32,88,128]{2,1,0:T(8,128)(2,1)}), bf16[32,88,128]{2,1,0:T(8,128)(2,1)S(1)}, u32[]{:S(2)}, u32[]{:S(2)}) async-start(bf16[32,88,128]{2,1,0:T(8,128)(2,1)} %broadcast_in_dim.8), calls=%async_computation.4 | async-start | bytes 1441792 | tf_op jit(solution)/shard_map/all_to_all | solution.py:34
  127.2 7.8 %all-to-all-start.5 = ((f32[2,256,64]{1,2,0:T(8,128)}), f32[2,256,64]{1,2,0:T(8,128)S(1)}, u32[]{:S(2)}, u32[]{:S(2)}) async-start(f32[2,256,64]{1,2,0:T(8,128)} %bitcast.147), calls=%async_computation.5 | async-start | bytes 262144 | tf_op jit(solution)/shard_map/all_to_all | solution.py:34
  136.4 10.5 %copy-start.1 = (f32[8,21,4032]{2,0,1:T(8,128)S(1)}, f32[8,21,4032]{2,0,1:T(8,128)}, u32[]{:S(2)}) copy-start(f32[8,21,4032]{2,0,1:T(8,128)} %param.8) | copy-start | bytes 8128516
